TPU v7x, 32 devices: a whole 2x2x4 slice. The times are simulated.
32 devices in a mesh: groups: 2 (over x), row: 16 (over z, y, core).
Axes of the slice: x: 2, y: 2, z: 4, core: 2. Of those that a mesh axis runs over, the one named last changes fastest.
Arguments:
- design_matrix: bfloat16 [1024, 65536], P('groups', 'row'), parts along dimension 0, may hold values from -0.0546875 to 0.0546875
- targets: float32 [1024, 128], P(('groups', 'row')), parts along dimension 0, may hold values from -24 to 24
- linear: float32 [131072, 128], P(('groups', 'row')), parts along dimension 0, may hold values from -24 to 24
- diagonal: float32 [131072], P(('groups', 'row')), parts along dimension 0, may hold values from 0.1 to 2
- lower_code: int32 [131072, 128], P(('groups', 'row')), parts along dimension 0, may hold values from -192 to -17
- upper_code: int32 [131072, 128], P(('groups', 'row')), parts along dimension 0, may hold values from 16 to 191
Outputs:
- box_iterate: float32 [131072, 128], P(('groups', 'row')), parts along dimension 0
- scaled_dual: float32 [131072, 128], P(('groups', 'row')), parts along dimension 0
There are 2 independent parts, one for each index of `groups`. A program takes and returns all parts, laid end to end along the dimension named above; each array names one. Nothing has to cross between parts.
All inputs are finite; a program needn't handle non-finite values.
Results may differ from a plain program's by a relative error of at most 0.00033.
Values may be sent and summed in bfloat16 or wider, within the bound.
No kernel may reach another device: no remote copies, remote signals or barrier semaphores. Data moves between devices by JAX's collectives and lax.ppermute only.
A program may use at most 128 MiB of HBM per device.

v0:
```python
import jax
import jax.numpy as jnp
from jax import lax
from jax.sharding import PartitionSpec as P

ITERS = 4
rho_plus_lip = 7.0


def solve_small(matrix, rhs):
    count = len(rhs)
    table = [list(line) for line in matrix]
    right = list(rhs)
    for p in range(count):
        for i in range(p + 1, count):
            factor = table[i][p] / table[p][p]
            for j in range(p, count):
                table[i][j] = table[i][j] - factor * table[p][j]
            right[i] = right[i] - factor * right[p]
    result = [None] * count
    for i in reversed(range(count)):
        total = right[i]
        for j in range(i + 1, count):
            total = total - table[i][j] * result[j]
        result[i] = total / table[i][i]
    return result


def mix_weights(gram):
    count = len(gram)
    trace = gram[0][0]
    for i in range(1, count):
        trace = trace + gram[i][i]
    shift = 0.01 * trace / count + 1e-06
    matrix = [[gram[i][j] + (shift if i == j else 0.0) for j in range(count)] for i in range(count)]
    solved = solve_small(matrix, [jnp.ones_like(trace)] * count)
    total = solved[0]
    for i in range(1, count):
        total = total + solved[i]
    return [item / total for item in solved]


def apply_map(design_matrix, misfit, z, u, linear, diag, step_size, lower, upper):
    gradient = lax.dot_general(
        design_matrix, misfit, (((0,), (0,)), ((), ())), preferred_element_type=jnp.float32
    )
    point = z - u
    gradient = gradient + diag * point + linear
    moved = point - step_size * gradient
    boxed = jnp.clip(moved + u, lower, upper)
    return (boxed, u + moved - boxed)


def per_device(design_matrix, targets, linear, diagonal, lower_code, upper_code):
    lower = lower_code.astype(jnp.float32) / 64.0
    upper = upper_code.astype(jnp.float32) / 64.0
    diag = diagonal[:, None]
    step_size = 1.0 / (rho_plus_lip + diag)
    z = jnp.zeros(linear.shape, jnp.float32)
    u = z
    mapped = []
    change = []
    gram = {}
    fresh = []
    for iteration in range(ITERS):
        if iteration == 0:
            misfit = (-targets).astype(jnp.bfloat16)
        else:
            product = lax.psum_scatter(
                jnp.dot(
                    design_matrix, (z - u).astype(jnp.bfloat16), preferred_element_type=jnp.float32
                ),
                "row",
                scatter_dimension=0,
                tiled=True,
            )
            misfit = (product - targets).astype(jnp.bfloat16)
        misfit = lax.all_gather(misfit, "row", axis=0, tiled=True)
        boxed, scaled = apply_map(
            design_matrix, misfit, z, u, linear, diag, step_size, lower, upper
        )
        mapped.append((boxed, scaled))
        change.append((boxed - z, scaled - u))
        for i in range(iteration + 1):
            fresh.append(
                (
                    (i, iteration),
                    jnp.sum(
                        change[i][0] * change[iteration][0] + change[i][1] * change[iteration][1],
                        axis=0,
                    ),
                )
            )
        if iteration == 0:
            z, u = (boxed, scaled)
            continue
        partial = jnp.stack([item for _, item in fresh])
        whole = jnp.sum(lax.all_gather(partial, "row", axis=0), axis=0)
        for k, (pair, _) in enumerate(fresh):
            gram[pair] = whole[k]
        fresh = []
        count = iteration + 1
        alpha = mix_weights(
            [[gram[min(i, j), max(i, j)] for j in range(count)] for i in range(count)]
        )
        z = alpha[0][None, :] * mapped[0][0]
        u = alpha[0][None, :] * mapped[0][1]
        for i in range(1, count):
            z = z + alpha[i][None, :] * mapped[i][0]
            u = u + alpha[i][None, :] * mapped[i][1]
        z = jnp.clip(z, lower, upper)
    return (z, u)


def solution(mesh):
    in_specs = (
        P("groups", "row"),
        P(("groups", "row"), None),
        P(("groups", "row"), None),
        P(("groups", "row")),
        P(("groups", "row"), None),
        P(("groups", "row"), None),
    )
    out_specs = (P(("groups", "row"), None), P(("groups", "row"), None))
    return jax.shard_map(
        per_device, mesh=mesh, in_specs=in_specs, out_specs=out_specs, check_vma=False
    )
```

profile of v0, /device:TPU:0, one launch (start us, length us, event | category | flops | bytes accessed | tf_op | source)
XLA Modules:
  0.0 378.7 jit_solution(17872735415210531985)
XLA Ops:
  7.2 0.0 reduce-scatter.4.cloned.1.call-start
  7.2 0.7 negate_convert_fusion
  7.9 0.7 add_divide_fusion
  8.7 23.5 %all_gather.30 = bf16[512,128]{1,0:T(8,128)(2,1)S(1)} all-gather(bf16[32,128]{1,0:T(8,128)(2,1)S(1)} %negate_convert_fusion), channel_id=1, replica_groups=mesh['groups'=2,'row'=16] {'row'}, dimensions={0}, use_global_device_ids=true | all-gather | bytes 139264 | tf_op jit(solution)/shard_map/all_gather | solution.py:78
  32.1 6.4 %fusion.52 = (f32[4096,128]{1,0:T(8,128)S(1)}, f32[4096,128]{1,0:T(8,128)}, f32[4096,128]{1,0:T(8,128)S(1)}) fusion(s32[4096,128]{1,0:T(8,128)} %param.10, s32[4096,128]{1,0:T(8,128)} %param.11, f32[4096,128]{1,0:T(8,128)} %param.8, f32[4096]{0:T(1024)S(1)} %get-tuple-element.64, bf16[512,4096]{1,0:T(8,128)(2,1)} %param.6, ...), kind=kOutput, calls=%fused_computation.132 | convolution fusion | flops 543162368 | bytes 16941056 | tf_op jit(solution)/shard_map/dot_general | solution.py:44
  38.5 1.3 copy-done.6
  39.8 1.9 convolution_bitcast_fusion.5
  41.8 0.0 reduce-scatter.4.cloned.1.call-update
  41.8 0.0 reduce-scatter.6.cloned.1.call-start
  41.8 53.1 %reduce-scatter.4.cloned.1.call-done = f32[32,128]{1,0:T(8,128)} async-done(((f32[512,128]{1,0:T(8,128)}), f32[32,128]{1,0:T(8,128)}) %reduce-scatter.4.cloned.1.call-update) | async-done | bytes 16400 | tf_op jit(solution)/shard_map/reduce_scatter | solution.py:69
  94.9 0.7 subtract_convert_fusion.2
  95.6 19.7 %all_gather.31 = bf16[512,128]{1,0:T(8,128)(2,1)S(1)} all-gather(bf16[32,128]{1,0:T(8,128)(2,1)S(1)} %subtract_convert_fusion.2), channel_id=1, replica_groups=mesh['groups'=2,'row'=16] {'row'}, dimensions={0}, use_global_device_ids=true | all-gather | bytes 139264 | tf_op jit(solution)/shard_map/all_gather | solution.py:78
  115.4 8.5 %add_reduce_fusion.9 = (f32[128]{0:T(128)S(1)}, f32[128]{0:T(128)S(1)}, f32[128]{0:T(128)S(1)}, f32[4096,128]{1,0:T(8,128)}, f32[4096,128]{1,0:T(8,128)}, /*index=5*/f32[4096,128]{1,0:T(8,128)}) fusion(f32[4096,128]{1,0:T(8,128)} %get-tuple-element.57, f32[4096,128]{1,0:T(8,128)S(1)} %get-tuple-element.58, s32[4096,128]{1,0:T(8,128)} %param.10, ...), kind=kOutput, calls=%fused_computation.40 | convolution fusion | flops 551026304 | bytes 23234048 | tf_op jit(solution)/shard_map/dot_general | solution.py:44
  123.9 17.5 %all-gather.3 = f32[16,3,128]{2,1,0:T(4,128)S(1)} all-gather(f32[1,3,128]{2,1,0:T(4,128)S(1)} %maximum_bitcast_fusion), channel_id=2, replica_groups=mesh['groups'=2,'row'=16] {'row'}, dimensions={0}, use_global_device_ids=true | all-gather | bytes 26112 | tf_op jit(solution)/shard_map/all_gather | solution.py:98
  141.5 6.9 %convolution_bitcast_fusion.4 = f32[512,128]{1,0:T(8,128)} fusion(bf16[512,4096]{1,0:T(8,128)(2,1)} %param.6, f32[4096,128]{1,0:T(8,128)} %get-tuple-element.70, f32[128]{0:T(128)S(1)} %fusion.24, f32[4096,128]{1,0:T(8,128)S(1)} %get-tuple-element.58, f32[128]{0:T(128)S(1)} %get-tuple-element.48, s32[4096,128]{1,0:T(8,128)} %param.10, ...), kind=kOutput, calls=%fused_computation.45 | convolution fusion | flops 545783808 | bytes 14943232 | tf_op jit(solution)/shard_map/dot_general | solution.py:70
  148.4 0.0 reduce-scatter.8.cloned.1.call-start
  148.5 54.2 %reduce-scatter.6.cloned.1.call-done = f32[32,128]{1,0:T(8,128)} async-done(((f32[512,128]{1,0:T(8,128)}), f32[32,128]{1,0:T(8,128)}) %reduce-scatter.6.cloned.1.call-update) | async-done | bytes 16400 | tf_op jit(solution)/shard_map/reduce_scatter | solution.py:69
  202.7 0.7 subtract_convert_fusion.1
  203.4 19.8 %all_gather.34 = bf16[512,128]{1,0:T(8,128)(2,1)S(1)} all-gather(bf16[32,128]{1,0:T(8,128)(2,1)S(1)} %subtract_convert_fusion.1), channel_id=1, replica_groups=mesh['groups'=2,'row'=16] {'row'}, dimensions={0}, use_global_device_ids=true | all-gather | bytes 139264 | tf_op jit(solution)/shard_map/all_gather | solution.py:78
  223.2 10.1 %add_reduce_fusion.6 = (f32[128]{0:T(128)S(1)}, f32[128]{0:T(128)S(1)}, f32[128]{0:T(128)S(1)}, f32[4096,128]{1,0:T(8,128)}, f32[4096,128]{1,0:T(8,128)}, /*index=5*/f32[4096,128]{1,0:T(8,128)}) fusion(f32[4096,128]{1,0:T(8,128)} %get-tuple-element.57, f32[4096,128]{1,0:T(8,128)S(1)} %get-tuple-element.58, f32[4096,128]{1,0:T(8,128)} %get-tuple-element.55, ...), kind=kOutput, calls=%fused_computation.33 | convolution fusion | flops 557317760 | bytes 27429376 | tf_op jit(solution)/shard_map/dot_general | solution.py:44
  233.3 17.7 %all-gather.4 = f32[16,3,128]{2,1,0:T(4,128)S(1)} all-gather(f32[1,3,128]{2,1,0:T(4,128)S(1)} %maximum_bitcast_fusion.1), channel_id=3, replica_groups=mesh['groups'=2,'row'=16] {'row'}, dimensions={0}, use_global_device_ids=true | all-gather | bytes 26112 | tf_op jit(solution)/shard_map/all_gather | solution.py:98
  251.1 7.1 %fusion.33 = (f32[4096,128]{1,0:T(8,128)S(1)}, f32[4096,128]{1,0:T(8,128)}) fusion(f32[128]{0:T(128)S(1)} %get-tuple-element.69, f32[128]{0:T(128)S(1)} %get-tuple-element.68, f32[4096,128]{1,0:T(8,128)S(1)} %get-tuple-element.58, f32[128]{0:T(128)S(1)} %get-tuple-element.36, s32[4096,128]{1,0:T(8,128)} %param.10, s32[4096,128]{1,0:T(8,128)} %param.11, ...), kind=kLoop, calls=%fused_computation.112 | loop fusion | flops 12058624 | bytes 16778752 | tf_op jit(solution)/shard_map/sub | solution.py:47
  258.2 1.3 copy-done.5
  259.5 2.0 convolution_bitcast_fusion.3
  261.5 54.2 %reduce-scatter.8.cloned.1.call-done = f32[32,128]{1,0:T(8,128)} async-done(((f32[512,128]{1,0:T(8,128)}), f32[32,128]{1,0:T(8,128)}) %reduce-scatter.8.cloned.1.call-update) | async-done | bytes 16400 | tf_op jit(solution)/shard_map/reduce_scatter | solution.py:69
  315.8 0.7 subtract_convert_fusion
  316.5 19.7 %all_gather.37 = bf16[512,128]{1,0:T(8,128)(2,1)S(1)} all-gather(bf16[32,128]{1,0:T(8,128)(2,1)S(1)} %subtract_convert_fusion), channel_id=1, replica_groups=mesh['groups'=2,'row'=16] {'row'}, dimensions={0}, use_global_device_ids=true | all-gather | bytes 139264 | tf_op jit(solution)/shard_map/all_gather | solution.py:78
  336.3 9.4 %fusion.22 = (f32[4096,128]{1,0:T(8,128)S(1)}, f32[4096,128]{1,0:T(8,128)S(1)}, f32[4096,128]{1,0:T(8,128)}) fusion(s32[4096,128]{1,0:T(8,128)} %param.10, s32[4096,128]{1,0:T(8,128)} %param.11, f32[128]{0:T(128)S(1)} %get-tuple-element.69, f32[128]{0:T(128)S(1)} %get-tuple-element.68, f32[4096,128]{1,0:T(8,128)S(1)} %get-tuple-element.58, ...), kind=kOutput, calls=%fused_computation.51 | convolution fusion | flops 550502400 | bytes 27428352 | tf_op jit(solution)/shard_map/dot_general | solution.py:44
  345.7 0.8 copy-done.8
  346.5 1.1 add_reduce_fusion.3
  347.6 17.5 %all-gather.5 = f32[16,4,128]{2,1,0:T(4,128)S(1)} all-gather(f32[1,4,128]{2,1,0:T(4,128)S(1)} %maximum_bitcast_fusion.2), channel_id=4, replica_groups=mesh['groups'=2,'row'=16] {'row'}, dimensions={0}, use_global_device_ids=true | all-gather | bytes 34816 | tf_op jit(solution)/shard_map/all_gather | solution.py:98
  365.3 6.9 %multiply_add_fusion = (f32[4096,128]{1,0:T(8,128)}, f32[4096,128]{1,0:T(8,128)}) fusion(f32[4096,128]{1,0:T(8,128)} %get-tuple-element.57, f32[128]{0:T(128)S(1)} %get-tuple-element.67, f32[128]{0:T(128)S(1)} %get-tuple-element.66, f32[128]{0:T(128)S(1)} %get-tuple-element.65, f32[128]{0:T(128)S(1)} %get-tuple-element.12, ...), kind=kLoop, calls=%fused_computation.22 | loop fusion | flops 15204352 | bytes 18876416 | tf_op jit(solution)/shard_map/add | solution.py:110
  (38 shorter events, 0.4 us)
Async XLA Ops:
  7.2 87.7 %reduce-scatter.4.cloned.1.call-start = ((), (), s32[]{:S(2)}) async-start(), calls=%async_computation.3 | async-start | bytes 278528 | tf_op jit(solution)/shard_map/reduce_scatter | solution.py:69
  32.1 7.7 %copy-start = (bf16[512,4096]{1,0:T(8,128)(2,1)S(1)}, bf16[512,4096]{1,0:T(8,128)(2,1)}, u32[]{:S(2)}) copy-start(bf16[512,4096]{1,0:T(8,128)(2,1)} %param.6) | copy-start | bytes 12582916
  38.5 1.3 copy-start.6
  39.8 55.1 %copy-start.10 = (f32[32,128]{1,0:T(8,128)S(1)}, f32[32,128]{1,0:T(8,128)}, u32[]{:S(2)}) copy-start(f32[32,128]{1,0:T(8,128)} %param.7) | copy-start | bytes 49156
  39.8 75.6 %copy-start.9 = (f32[4096]{0:T(1024)S(1)}, f32[4096]{0:T(1024)}, u32[]{:S(2)}) copy-start(f32[4096]{0:T(1024)} %param.9) | copy-start | bytes 49156
  41.8 160.9 %reduce-scatter.6.cloned.1.call-start = ((), (), s32[]{:S(2)}) async-start(), calls=%async_computation.4 | async-start | bytes 278528 | tf_op jit(solution)/shard_map/reduce_scatter | solution.py:69
  148.4 167.4 %reduce-scatter.8.cloned.1.call-start = ((), (), s32[]{:S(2)}) async-start(), calls=%async_computation.5 | async-start | bytes 278528 | tf_op jit(solution)/shard_map/reduce_scatter | solution.py:69
  251.1 8.5 %copy-start.1 = (bf16[512,4096]{1,0:T(8,128)(2,1)S(1)}, bf16[512,4096]{1,0:T(8,128)(2,1)}, u32[]{:S(2)}) copy-start(bf16[512,4096]{1,0:T(8,128)(2,1)} %param.6) | copy-start | bytes 12582916
  258.2 1.3 copy-start.5
  336.3 9.4 %copy-start.2 = (f32[4096,128]{1,0:T(8,128)S(1)}, f32[4096,128]{1,0:T(8,128)}, u32[]{:S(2)}) copy-start(f32[4096,128]{1,0:T(8,128)} %get-tuple-element.57) | copy-start | bytes 6291460
  336.3 9.4 %copy-start.3 = (f32[4096,128]{1,0:T(8,128)S(1)}, f32[4096,128]{1,0:T(8,128)}, u32[]{:S(2)}) copy-start(f32[4096,128]{1,0:T(8,128)} %get-tuple-element.54) | copy-start | bytes 6291460
  336.3 9.4 %copy-start.4 = (f32[4096,128]{1,0:T(8,128)S(1)}, f32[4096,128]{1,0:T(8,128)}, u32[]{:S(2)}) copy-start(f32[4096,128]{1,0:T(8,128)} %get-tuple-element.55) | copy-start | bytes 6291460
  336.3 9.5 %copy-start.7 = (f32[4096,128]{1,0:T(8,128)S(1)}, f32[4096,128]{1,0:T(8,128)}, u32[]{:S(2)}) copy-start(f32[4096,128]{1,0:T(8,128)} %get-tuple-element.46) | copy-start | bytes 6291460
  336.3 10.3 %copy-start.8 = (f32[4096,128]{1,0:T(8,128)S(1)}, f32[4096,128]{1,0:T(8,128)}, u32[]{:S(2)}) copy-start(f32[4096,128]{1,0:T(8,128)} %get-tuple-element.47) | copy-start | bytes 6291460
Sparse Core Ops, SparseCore 0:
  41.9 52.9 reduce-scatter.3
  148.5 54.1 reduce-scatter.5
  261.7 54.0 reduce-scatter.7
where the time goes:
time: 379 us
  waiting for transfers between devices  162 us (43%)
  blocking collectives  135 us (36%)
  matrix products  45.2 us (12%)
  other arithmetic  19.1 us (5%)
  between operations  13.9 us (4%)
    reduce_scatter x3, waiting for transfers between devices, per_device(): lax.psum_scatter(jnp.dot(design_matrix, (z - u).astype(jnp.bfloat16), pre...  162 us
    all_gather x4, blocking collectives, per_device(): misfit = lax.all_gather(misfit, 'row', axis=0, tiled=True)  82.7 us
    all_gather x3, blocking collectives, per_device(): whole = jnp.sum(lax.all_gather(partial, 'row', axis=0), axis=0)  52.7 us
    dot_general x4, matrix products, apply_map(): lax.dot_general(design_matrix, misfit, (((0,), (0,)), ((), ())), preferre...  34.4 us
    dot_general x3, matrix products, per_device(): jnp.dot(design_matrix, (z - u).astype(jnp.bfloat16), preferred_element_ty...  10.8 us
  transfers between devices with their start and end apart: 3, of which 3 were waited for; matrix products, arithmetic and copies ran while one was open for 0% of the time, Pallas kernels for 0%

commit v1 on v0

--- a/solution.py
+++ b/solution.py
@@ -75,7 +75,20 @@
                 tiled=True,
             )
             misfit = (product - targets).astype(jnp.bfloat16)
-        misfit = lax.all_gather(misfit, "row", axis=0, tiled=True)
+
+        def number_record_on_mesh(target, a_name):
+            dev_count = lax.axis_size(a_name)
+            d_next = [None] * dev_count
+            d_next[dev_count - 1] = target
+            in_order = [(rr, (rr + 1) % dev_count) for rr in range(dev_count)]
+            for dev_j in range(dev_count - 2, -1, -1):
+                d_next[dev_j] = lax.ppermute(d_next[dev_j + 1], a_name, in_order)
+            main = jnp.concatenate(d_next, 0)
+            local_out = lax.axis_index(a_name)
+            tmp = jnp.roll(main, (local_out + 1) * target.shape[0], 0)
+            return tmp
+
+        misfit = number_record_on_mesh(misfit, "row")
         boxed, scaled = apply_map(
             design_matrix, misfit, z, u, linear, diag, step_size, lower, upper
         )

time: 379 us -> 676 us (1.78)
  waiting for transfers between devices: 162 us -> 519 us
  blocking collectives: 135 us -> 51.8 us
  local copies, waits for them, and re-layouts: 3.48 us -> 21.9 us
    ppermute x0 -> x60, waiting for transfers between devices: none -> 353 us  [number_record_on_mesh(): d_next[dev_j] = lax.ppermute(d_next[dev_j + 1], a_name, in_order)]
    unnamed x3 -> x6, waiting for transfers between devices: 0.05 us -> 166 us
    reduce_scatter x3 -> x0, waiting for transfers between devices: 162 us -> none  [per_device(): lax.psum_scatter(jnp.dot(design_matrix, (z - u).astype(jnp.bfloat16), pre...]
    all_gather x4 -> x0, blocking collectives: 82.7 us -> none  [per_device(): misfit = lax.all_gather(misfit, 'row', axis=0, tiled=True)]
    unnamed x22 -> x53, local copies, waits for them, and re-layouts: 3.48 us -> 21.3 us
  transfers between devices with their start and end apart: 3 -> 63, of which waited for: 3 -> 62; matrix products, arithmetic and copies ran while one was open for 0% -> 1% of each run, Pallas kernels for 0% -> 0%
where the time goes in v1:
time: 676 us; the launch traced here: 675 us
  waiting for transfers between devices  519 us (77%)
  blocking collectives  51.8 us (8%)
  matrix products  49.8 us (7%)
  local copies, waits for them, and re-layouts  21.9 us (3%)
  other arithmetic  17.7 us (3%)
  between operations  14.1 us (2%)
    ppermute x60, waiting for transfers between devices, number_record_on_mesh(): d_next[dev_j] = lax.ppermute(d_next[dev_j + 1], a_name, in_order)  353 us
    unnamed x6, waiting for transfers between devices  166 us
    all_gather x3, blocking collectives, per_device(): whole = jnp.sum(lax.all_gather(partial, 'row', axis=0), axis=0)  51.8 us
    dot_general x4, matrix products, apply_map(): lax.dot_general(design_matrix, misfit, (((0,), (0,)), ((), ())), preferre...  40.3 us
    unnamed x53, local copies, waits for them, and re-layouts  21.3 us
  transfers between devices with their start and end apart: 63, of which 62 were waited for; matrix products, arithmetic and copies ran while one was open for 1% of the time, Pallas kernels for 0%

profile of v1, /device:TPU:0, one launch (start us, length us, event | category | flops | bytes accessed | tf_op | source)
XLA Modules:
  0.0 675.5 jit_solution(9387571026774067223)
XLA Ops:
  8.4 6.3 collective-permute-done
  98.4 7.5 %fusion.69 = (f32[4096,128]{0,1:T(8,128)S(1)}, f32[4096,128]{0,1:T(8,128)}, f32[4096,128]{0,1:T(8,128)}) fusion(s32[4096,128]{0,1:T(8,128)S(1)} %copy.20, s32[4096,128]{0,1:T(8,128)} %copy.19, f32[4096,128]{0,1:T(8,128)} %copy.21, f32[4096]{0:T(1024)S(1)} %get-tuple-element.69, bf16[512,4096]{1,0:T(8,128)(2,1)} %param.8, s32[]{:T(128)S(6)} %select_n.17, ...), kind=kOutput, calls=%fused_computation.169 | convolution fusion | flops 543424512 | bytes 16941060 | tf_op jit(solution)/shard_map/dot_general | solution.py:44
  109.9 57.4 %reduce-scatter.10.cloned.1.call-done = f32[32,128]{1,0:T(8,128)} async-done(((f32[512,128]{1,0:T(8,128)}), f32[32,128]{1,0:T(8,128)}) %reduce-scatter.10.cloned.1.call-update) | async-done | bytes 16400
  174.1 6.0 collective-permute-done.16
  180.2 6.0 collective-permute-done.17
  186.2 6.0 collective-permute-done.18
  192.3 6.0 collective-permute-done.19
  198.3 6.0 collective-permute-done.20
  204.3 6.0 collective-permute-done.21
  210.4 6.0 collective-permute-done.22
  216.4 6.0 collective-permute-done.23
  222.4 6.0 collective-permute-done.24
  228.5 6.0 collective-permute-done.25
  234.5 6.0 collective-permute-done.26
  240.6 6.0 collective-permute-done.27
  258.9 10.4 %add_reduce_fusion.9 = (f32[128]{0:T(128)S(1)}, f32[128]{0:T(128)S(1)}, f32[128]{0:T(128)S(1)}, f32[4096,128]{0,1:T(8,128)}, f32[4096,128]{0,1:T(8,128)}, /*index=5*/f32[4096,128]{0,1:T(8,128)}) fusion(f32[4096,128]{0,1:T(8,128)} %get-tuple-element.62, f32[4096,128]{0,1:T(8,128)} %get-tuple-element.63, s32[4096,128]{0,1:T(8,128)S(1)} %copy.20, ...), kind=kOutput, calls=%fused_computation.41 | convolution fusion | flops 551288448 | bytes 23234052 | tf_op jit(solution)/shard_map/dot_general | solution.py:44
  269.4 17.4 %all-gather.3 = f32[16,3,128]{2,1,0:T(4,128)S(1)} all-gather(f32[1,3,128]{2,1,0:T(4,128)S(1)} %maximum_bitcast_fusion), channel_id=2, replica_groups=mesh['groups'=2,'row'=16] {'row'}, dimensions={0}, use_global_device_ids=true | all-gather | bytes 26112 | tf_op jit(solution)/shard_map/all_gather | solution.py:111
  286.8 6.4 convolution_bitcast_fusion.4
  294.2 54.5 %reduce-scatter.12.cloned.1.call-done = f32[32,128]{1,0:T(8,128)} async-done(((f32[512,128]{1,0:T(8,128)}), f32[32,128]{1,0:T(8,128)}) %reduce-scatter.12.cloned.1.call-update) | async-done | bytes 16400
  379.7 6.0 collective-permute-done.35
  391.8 6.0 collective-permute-done.37
  422.0 6.0 collective-permute-done.42
  440.4 12.3 %add_reduce_fusion.6 = (f32[128]{0:T(128)S(1)}, f32[128]{0:T(128)S(1)}, f32[128]{0:T(128)S(1)}, f32[4096,128]{0,1:T(8,128)}, f32[4096,128]{0,1:T(8,128)}, /*index=5*/f32[4096,128]{0,1:T(8,128)}) fusion(f32[4096,128]{0,1:T(8,128)} %get-tuple-element.62, f32[4096,128]{0,1:T(8,128)} %get-tuple-element.63, f32[4096,128]{0,1:T(8,128)} %get-tuple-element.60, ...), kind=kOutput, calls=%fused_computation.34 | convolution fusion | flops 557579904 | bytes 27429380 | tf_op jit(solution)/shard_map/dot_general | solution.py:44
  452.7 17.2 %all-gather.4 = f32[16,3,128]{2,1,0:T(4,128)S(1)} all-gather(f32[1,3,128]{2,1,0:T(4,128)S(1)} %maximum_bitcast_fusion.1), channel_id=3, replica_groups=mesh['groups'=2,'row'=16] {'row'}, dimensions={0}, use_global_device_ids=true | all-gather | bytes 26112 | tf_op jit(solution)/shard_map/all_gather | solution.py:111
  470.0 7.3 %fusion.50 = (f32[4096,128]{0,1:T(8,128)S(1)}, f32[4096,128]{0,1:T(8,128)}) fusion(f32[128]{0:T(128)S(1)} %get-tuple-element.74, f32[128]{0:T(128)S(1)} %get-tuple-element.73, f32[4096,128]{0,1:T(8,128)} %get-tuple-element.63, f32[128]{0:T(128)S(1)} %get-tuple-element.41, s32[4096,128]{0,1:T(8,128)S(1)} %copy.20, s32[4096,128]{0,1:T(8,128)} %copy.19, ...), kind=kLoop, calls=%fused_computation.149 | loop fusion | flops 12058624 | bytes 16778752 | tf_op jit(solution)/shard_map/sub | solution.py:47
  481.1 54.5 %reduce-scatter.14.cloned.1.call-done = f32[32,128]{1,0:T(8,128)} async-done(((f32[512,128]{1,0:T(8,128)}), f32[32,128]{1,0:T(8,128)}) %reduce-scatter.14.cloned.1.call-update) | async-done | bytes 16400
  548.6 6.0 collective-permute-done.47
  578.7 6.0 collective-permute-done.52
  590.8 6.0 collective-permute-done.54
  627.3 10.0 %fusion.31 = (f32[4096,128]{0,1:T(8,128)S(1)}, f32[4096,128]{0,1:T(8,128)S(1)}, f32[4096,128]{0,1:T(8,128)}) fusion(s32[4096,128]{0,1:T(8,128)S(1)} %copy.20, s32[4096,128]{0,1:T(8,128)} %copy.19, f32[128]{0:T(128)S(1)} %get-tuple-element.74, f32[128]{0:T(128)S(1)} %get-tuple-element.73, f32[4096,128]{0,1:T(8,128)} %get-tuple-element.63, ...), kind=kOutput, calls=%fused_computation.67 | convolution fusion | flops 550764544 | bytes 27428356 | tf_op jit(solution)/shard_map/dot_general | solution.py:44
  639.7 17.2 %all-gather.5 = f32[16,4,128]{2,1,0:T(4,128)S(1)} all-gather(f32[1,4,128]{2,1,0:T(4,128)S(1)} %maximum_bitcast_fusion.2), channel_id=4, replica_groups=mesh['groups'=2,'row'=16] {'row'}, dimensions={0}, use_global_device_ids=true | all-gather | bytes 34816 | tf_op jit(solution)/shard_map/all_gather | solution.py:111
  657.0 7.0 %multiply_add_fusion = (f32[4096,128]{0,1:T(8,128)}, f32[4096,128]{0,1:T(8,128)}) fusion(f32[4096,128]{0,1:T(8,128)} %get-tuple-element.62, f32[128]{0:T(128)S(1)} %get-tuple-element.72, f32[128]{0:T(128)S(1)} %get-tuple-element.71, f32[128]{0:T(128)S(1)} %get-tuple-element.70, f32[128]{0:T(128)S(1)} %get-tuple-element.17, ...), kind=kLoop, calls=%fused_computation.23 | loop fusion | flops 15204352 | bytes 18876416 | tf_op jit(solution)/shard_map/add | solution.py:123
  (189 shorter events, 267.2 us)
Async XLA Ops:
  7.2 160.1 %reduce-scatter.10.cloned.1.call-start = ((), (), s32[]{:S(2)}) async-start(), calls=%async_computation.3 | async-start | bytes 278528
  7.9 6.8 %collective-permute-start = (bf16[32,128]{1,0:T(8,128)(2,1)S(1)}, bf16[32,128]{1,0:T(8,128)(2,1)S(1)}, u32[]{:S(2)}, u32[]{:S(2)}) collective-permute-start(bf16[32,128]{1,0:T(8,128)(2,1)S(1)} %negate_convert_fusion), channel_id=1, source_target_pairs={{0,1},{1,2},{2,3},{3,4},{4,5},{5,6},{6,7},{7,8},{8,9},{9,10},{10,1... | collective-permute-start | bytes 24584 | tf_op jit(solution)/shard_map/ppermute | solution.py:85
  89.8 8.4 %collective-permute-start.14 = (bf16[32,128]{1,0:T(8,128)(2,1)S(1)}, bf16[32,128]{1,0:T(8,128)(2,1)S(1)}, u32[]{:S(2)}, u32[]{:S(2)}) collective-permute-start(bf16[32,128]{1,0:T(8,128)(2,1)S(1)} %collective-permute-done.13), channel_id=1, source_target_pairs={{0,1},{1,2},{2,3},{3,4},{4,5},{5,6},{6,7},{7,8},{8,9},{9,10},{10,1... | collective-permute-start | bytes 24584 | tf_op jit(solution)/shard_map/ppermute | solution.py:85
  109.7 238.9 %reduce-scatter.12.cloned.1.call-start = ((), (), s32[]{:S(2)}) async-start(), calls=%async_computation.4 | async-start | bytes 278528
  168.1 6.1 collective-permute-start.15
  174.1 6.0 collective-permute-start.16
  180.2 6.0 collective-permute-start.17
  186.2 6.0 collective-permute-start.18
  192.3 6.0 collective-permute-start.19
  198.3 6.0 collective-permute-start.20
  204.3 6.0 collective-permute-start.21
  210.4 6.0 collective-permute-start.22
  216.4 6.0 collective-permute-start.23
  222.4 6.0 collective-permute-start.24
  228.5 6.0 collective-permute-start.25
  234.5 6.0 collective-permute-start.26
  240.6 6.0 collective-permute-start.27
  246.6 6.0 collective-permute-start.28
  252.6 6.0 collective-permute-start.29
  294.1 241.5 %reduce-scatter.14.cloned.1.call-start = ((), (), s32[]{:S(2)}) async-start(), calls=%async_computation.5 | async-start | bytes 278528
  349.5 6.1 collective-permute-start.30
  355.6 6.0 collective-permute-start.31
  361.6 6.0 collective-permute-start.32
  367.7 6.0 collective-permute-start.33
  373.7 6.0 collective-permute-start.34
  379.7 6.0 collective-permute-start.35
  385.8 6.0 collective-permute-start.36
  391.8 6.0 collective-permute-start.37
  536.4 6.1 collective-permute-start.45
  548.6 6.0 collective-permute-start.47
  590.8 6.0 collective-permute-start.54
  621.0 6.0 collective-permute-start.59
  (44 other events, 423.0 us)
Sparse Core Ops, SparseCore 0:
  109.8 57.3 reduce-scatter.9
  294.3 54.3 reduce-scatter.11
  481.2 54.3 reduce-scatter.13
